TPU v7x, 32 devices: a whole 2x2x4 slice. The times are simulated.
32 devices in a mesh: row: 4 (over z), col: 8 (over y, x, core).
Axes of the slice: x: 2, y: 2, z: 4, core: 2. Of those that a mesh axis runs over, the one named last changes fastest.
Arguments:
- x_blocks: bfloat16 [1024, 1024, 128], P('row', 'col'), may hold values from -0.0625 to 0.0625
- block_ids: int32 [1024, 8], P('row', 'col'), may hold values from 0 to 511, as said below
- margins: float32 [16384], P('row'), may hold values from -6 to 6
- deleted: int32 [2048], P('row'), may hold values from 0 to 16383, as said below
- grads: float32 [16384, 128], P('col'), may hold values from -6 to 6
Outputs:
- solution: float32 [16384, 128], P('col')
- residual: float32 [16384, 128], P('col')
Inputs may be any that keep to these rules, and one draw needn't show every extreme that they name: `block_ids`: each device's 256 entries are distinct and rise; each device lists the first and the last block of its grid. `deleted`: the 512 entries of row shard r are distinct rows of that shard, r * 4096 and up; each shard deletes its first and its last row.
All inputs are finite; a program needn't handle non-finite values.
Results may differ from a plain program's by a relative error of at most 0.015.
Values may be sent and summed in bfloat16 or wider, within the bound.
No kernel may reach another device: no remote copies, remote signals or barrier semaphores. Data moves between devices by JAX's collectives and lax.ppermute only.
A program may use at most 128 MiB of HBM per device.

v0:
```python
import jax
import jax.numpy as jnp
from jax import lax
from jax.sharding import PartitionSpec as P

ITERS = 3
highest = lax.Precision.HIGHEST
ridge_weight = 0.2


def on_device(x_blocks, block_ids, margins, deleted, grads):
    block_width = x_blocks.shape[1]
    feature_rows = grads.shape[0]
    directions = grads.shape[1]
    row_count = margins.shape[0]
    row_blocks = row_count // block_width
    feature_blocks = feature_rows // block_width
    pattern = block_ids[:, 0]
    block_row = pattern // feature_blocks
    block_column = pattern % feature_blocks
    row_select = (block_row[:, None] == jnp.arange(row_blocks, dtype=jnp.int32)[None, :]).astype(
        jnp.float32
    )
    column_select = (
        block_column[:, None] == jnp.arange(feature_blocks, dtype=jnp.int32)[None, :]
    ).astype(jnp.float32)
    global_rows = lax.axis_index("row") * row_count + jnp.arange(row_count, dtype=jnp.int32)
    removed = jnp.any(global_rows[:, None] == deleted[None, :], axis=1)
    logistic = jax.nn.sigmoid(margins)
    weights_flat = jnp.where(removed, 0.0, logistic * (1.0 - logistic))
    weights = weights_flat.reshape(row_blocks, block_width, 1)
    share_rows = feature_rows // lax.axis_size("row")
    offset = lax.axis_index("row") * share_rows

    def own_rows(values):
        return lax.dynamic_slice_in_dim(values, offset, share_rows, 0)

    residual = grads
    solution = jnp.zeros_like(residual)
    direction = residual
    mine = own_rows(residual)
    norm_now = lax.psum(jnp.sum(mine * mine, axis=0), ("row", "col"))
    for iteration in range(ITERS):
        apply_rounded = direction.astype(jnp.bfloat16)
        picked_tiles = apply_rounded.reshape(feature_blocks, block_width, directions)[block_column]
        forward = jnp.einsum(
            "bij,bjk->bik", x_blocks, picked_tiles, preferred_element_type=jnp.float32
        )
        partial_rows = jnp.einsum("br,bik->rik", row_select, forward, precision=highest)
        projected = lax.psum(partial_rows, "col")
        scaled = (weights * projected).astype(jnp.bfloat16)
        picked_rows = scaled[block_row]
        backward = jnp.einsum(
            "bji,bjk->bik", x_blocks, picked_rows, preferred_element_type=jnp.float32
        )
        summed = jnp.einsum("bc,bik->cik", column_select, backward, precision=highest)
        hessian_image = (
            lax.psum(summed.reshape(feature_rows, directions), "row") + ridge_weight * direction
        )
        own_image = own_rows(hessian_image)
        own_residual = own_rows(residual)
        curvature, cross_term, image_square = lax.psum(
            (
                jnp.sum(own_rows(direction) * own_image, axis=0),
                jnp.sum(own_residual * own_image, axis=0),
                jnp.sum(own_image * own_image, axis=0),
            ),
            ("row", "col"),
        )
        step_size = norm_now / curvature
        norm_next = norm_now - 2.0 * step_size * cross_term + step_size * step_size * image_square
        solution = solution + step_size * direction
        residual = residual - step_size * hessian_image
        if iteration + 1 < ITERS:
            direction = residual + norm_next / norm_now * direction
            norm_now = norm_next
    return (solution, residual)


def solution(mesh):
    placed = (P("row", "col", None), P("row", "col"), P("row"), P("row"), P("col", None))
    return jax.shard_map(
        on_device,
        mesh=mesh,
        in_specs=placed,
        out_specs=(P("col", None), P("col", None)),
        check_vma=False,
    )
```

profile of v0, /device:TPU:0, one launch (start us, length us, event | category | flops | bytes accessed | tf_op | source)
XLA Modules:
  0.0 801.8 jit_solution(736054281682014846)
XLA Ops:
  17.8 12.8 %convolution_bitcast_fusion.5 = f32[256,128,128]{1,2,0:T(8,128)} fusion(bf16[256,128,128]{2,1,0:T(8,128)(2,1)} %gather_fusion, bf16[256,128,128]{2,1,0:T(8,128)(2,1)} %param.5), kind=kOutput, calls=%fused_computation.11 | convolution fusion | flops 1073741824 | bytes 33554432 | tf_op jit(solution)/shard_map/bij,bjk->bik/dot_general | solution.py:46
  30.6 17.5 %copy.24 = f32[256,128,128]{2,0,1:T(8,128)} copy(f32[256,128,128]{1,2,0:T(8,128)} %convolution_bitcast_fusion.5) | data formatting | bytes 33554432 | tf_op jit(solution)/shard_map/bij,bjk->bik/dot_general | solution.py:46
  48.1 10.8 %fusion.5 = f32[32,128,128]{2,0,1:T(8,128)} fusion(f32[256,128,128]{2,0,1:T(8,128)} %copy.24, s32[256]{0:T(256)S(1)} %bitcast.61), kind=kOutput, calls=%fused_computation.36 | convolution fusion | flops 1610620928 | bytes 18875392 | tf_op jit(solution)/shard_map/br,bik->rik/dot_general | solution.py:49
  60.9 62.7 %all-reduce.9.cloned.1.call-done = f32[32,128,128]{2,0,1:T(8,128)} async-done(((f32[32,128,128]{2,0,1:T(8,128)}), f32[32,128,128]{2,0,1:T(8,128)}) %all-reduce.9.cloned.1.call-update) | async-done | bytes 2097168 | tf_op jit(solution)/shard_map/psum | solution.py:50
  134.5 14.4 %convolution_bitcast_fusion.4 = f32[256,128,128]{1,2,0:T(8,128)} fusion(bf16[256,128,128]{2,1,0:T(8,128)(2,1)} %gather_fusion.1, bf16[256,128,128]{2,1,0:T(8,128)(2,1)} %param.5), kind=kOutput, calls=%fused_computation.10 | convolution fusion | flops 1073741824 | bytes 33554432 | tf_op jit(solution)/shard_map/bji,bjk->bik/dot_general | solution.py:53
  148.9 17.5 %copy.27 = f32[256,128,128]{2,0,1:T(8,128)} copy(f32[256,128,128]{1,2,0:T(8,128)} %convolution_bitcast_fusion.4) | data formatting | bytes 33554432 | tf_op jit(solution)/shard_map/bji,bjk->bik/dot_general | solution.py:53
  176.9 51.1 %all-reduce.11.cloned.1.call-done = f32[2048,128]{1,0:T(8,128)} async-done(((f32[2048,128]{1,0:T(8,128)}), f32[2048,128]{1,0:T(8,128)}) %all-reduce.11.cloned.1.call-update) | async-done | bytes 1048592 | tf_op jit(solution)/shard_map/psum | solution.py:58
  229.4 40.4 %all-reduce.1 = (f32[128]{0:T(128)S(1)}, f32[128]{0:T(128)S(1)}, f32[128]{0:T(128)S(1)}) all-reduce(f32[128]{0:T(128)S(1)} %get-tuple-element.7, f32[128]{0:T(128)S(1)} %get-tuple-element.6, f32[128]{0:T(128)S(1)} %get-tuple-element.5), channel_id=1, replica_groups=mesh['row'=4,'col'=8] {'row','col'}, use_global_device_ids=true, to_apply=%region_1.2 | all-reduce | flops 384 | bytes 3072 | tf_op jit(solution)/shard_map/psum | solution.py:42
  280.8 12.8 %convolution_bitcast_fusion.3 = f32[256,128,128]{1,2,0:T(8,128)} fusion(bf16[256,128,128]{2,1,0:T(8,128)(2,1)} %gather_fusion.2, bf16[256,128,128]{2,1,0:T(8,128)(2,1)} %param.5), kind=kOutput, calls=%fused_computation.9 | convolution fusion | flops 1073741824 | bytes 33554432 | tf_op jit(solution)/shard_map/bij,bjk->bik/dot_general | solution.py:46
  293.7 17.5 %copy.30 = f32[256,128,128]{2,0,1:T(8,128)} copy(f32[256,128,128]{1,2,0:T(8,128)} %convolution_bitcast_fusion.3) | data formatting | bytes 33554432 | tf_op jit(solution)/shard_map/bij,bjk->bik/dot_general | solution.py:46
  311.2 10.7 %fusion.3 = f32[32,128,128]{2,0,1:T(8,128)} fusion(f32[256,128,128]{2,0,1:T(8,128)} %copy.30, s32[256]{0:T(256)S(1)} %bitcast.62), kind=kOutput, calls=%fused_computation.35 | convolution fusion | flops 1610620928 | bytes 18875392 | tf_op jit(solution)/shard_map/br,bik->rik/dot_general | solution.py:49
  322.1 61.1 %all-reduce.13.cloned.1.call-done = f32[32,128,128]{2,0,1:T(8,128)} async-done(((f32[32,128,128]{2,0,1:T(8,128)}), f32[32,128,128]{2,0,1:T(8,128)}) %all-reduce.13.cloned.1.call-update) | async-done | bytes 2097168 | tf_op jit(solution)/shard_map/psum | solution.py:50
  394.2 14.4 %convolution_bitcast_fusion.2 = f32[256,128,128]{1,2,0:T(8,128)} fusion(bf16[256,128,128]{2,1,0:T(8,128)(2,1)} %gather_fusion.3, bf16[256,128,128]{2,1,0:T(8,128)(2,1)} %param.5), kind=kOutput, calls=%fused_computation.8 | convolution fusion | flops 1073741824 | bytes 33554432 | tf_op jit(solution)/shard_map/bji,bjk->bik/dot_general | solution.py:53
  408.6 17.5 %copy.33 = f32[256,128,128]{2,0,1:T(8,128)} copy(f32[256,128,128]{1,2,0:T(8,128)} %convolution_bitcast_fusion.2) | data formatting | bytes 33554432 | tf_op jit(solution)/shard_map/bji,bjk->bik/dot_general | solution.py:53
  436.5 51.1 %all-reduce.15.cloned.1.call-done = f32[2048,128]{1,0:T(8,128)} async-done(((f32[2048,128]{1,0:T(8,128)}), f32[2048,128]{1,0:T(8,128)}) %all-reduce.15.cloned.1.call-update) | async-done | bytes 1048592 | tf_op jit(solution)/shard_map/psum | solution.py:58
  489.9 40.2 %all-reduce = (f32[128]{0:T(128)S(1)}, f32[128]{0:T(128)S(1)}, f32[128]{0:T(128)S(1)}) all-reduce(f32[128]{0:T(128)S(1)} %get-tuple-element.3, f32[128]{0:T(128)S(1)} %get-tuple-element.4, f32[128]{0:T(128)S(1)} %get-tuple-element.2), channel_id=1, replica_groups=mesh['row'=4,'col'=8] {'row','col'}, use_global_device_ids=true, to_apply=%region_16.17 | all-reduce | flops 384 | bytes 3072 | tf_op jit(solution)/shard_map/psum | solution.py:62
  541.5 12.8 %convolution_bitcast_fusion.1 = f32[256,128,128]{1,2,0:T(8,128)} fusion(bf16[256,128,128]{2,1,0:T(8,128)(2,1)} %gather_fusion.4, bf16[256,128,128]{2,1,0:T(8,128)(2,1)} %param.5), kind=kOutput, calls=%fused_computation.7 | convolution fusion | flops 1073741824 | bytes 33554432 | tf_op jit(solution)/shard_map/bij,bjk->bik/dot_general | solution.py:46
  554.3 17.5 %copy.36 = f32[256,128,128]{2,0,1:T(8,128)} copy(f32[256,128,128]{1,2,0:T(8,128)} %convolution_bitcast_fusion.1) | data formatting | bytes 33554432 | tf_op jit(solution)/shard_map/bij,bjk->bik/dot_general | solution.py:46
  571.8 10.7 %fusion.1 = f32[32,128,128]{2,0,1:T(8,128)} fusion(f32[256,128,128]{2,0,1:T(8,128)} %copy.36, s32[256]{0:T(256)S(1)} %bitcast.63), kind=kOutput, calls=%fused_computation.34 | convolution fusion | flops 1610620928 | bytes 18875392 | tf_op jit(solution)/shard_map/br,bik->rik/dot_general | solution.py:49
  582.9 60.9 %all-reduce.17.cloned.1.call-done = f32[32,128,128]{2,0,1:T(8,128)} async-done(((f32[32,128,128]{2,0,1:T(8,128)}), f32[32,128,128]{2,0,1:T(8,128)}) %all-reduce.17.cloned.1.call-update) | async-done | bytes 2097168 | tf_op jit(solution)/shard_map/psum | solution.py:50
  654.8 14.4 %convolution_bitcast_fusion = f32[256,128,128]{1,2,0:T(8,128)} fusion(bf16[256,128,128]{2,1,0:T(8,128)(2,1)} %gather_fusion.5, bf16[256,128,128]{2,1,0:T(8,128)(2,1)} %param.5), kind=kOutput, calls=%fused_computation.6 | convolution fusion | flops 1073741824 | bytes 33554432 | tf_op jit(solution)/shard_map/bji,bjk->bik/dot_general | solution.py:53
  669.1 17.5 %copy.39 = f32[256,128,128]{2,0,1:T(8,128)} copy(f32[256,128,128]{1,2,0:T(8,128)} %convolution_bitcast_fusion) | data formatting | bytes 33554432 | tf_op jit(solution)/shard_map/bji,bjk->bik/dot_general | solution.py:53
  697.1 51.1 %all-reduce.19.cloned.1.call-done = f32[2048,128]{1,0:T(8,128)} async-done(((f32[2048,128]{1,0:T(8,128)}), f32[2048,128]{1,0:T(8,128)}) %all-reduce.19.cloned.1.call-update) | async-done | bytes 1048592 | tf_op jit(solution)/shard_map/psum | solution.py:58
  751.0 40.0 %psum.106 = f32[128]{0:T(128)S(1)} all-reduce(f32[128]{0:T(128)S(1)} %multiply_reduce_fusion), channel_id=1, replica_groups=mesh['row'=4,'col'=8] {'row','col'}, use_global_device_ids=true, to_apply=%region_20.21 | all-reduce | flops 128 | bytes 1024 | tf_op jit(solution)/shard_map/psum | solution.py:62
  (59 shorter events, 109.9 us)
Async XLA Ops:
  7.2 116.4 %all-reduce.9.cloned.1.call-start = ((), (), s32[]{:S(2)}) async-start(), calls=%async_computation | async-start | bytes 4194304 | tf_op jit(solution)/shard_map/psum | solution.py:50
  48.1 11.1 %copy-start.3 = (s32[512]{0:T(512)S(1)}, s32[512]{0:T(512)}, u32[]{:S(2)}) copy-start(s32[512]{0:T(512)} %param.8) | copy-start | bytes 6148
  48.1 12.6 %copy-start.2 = (f32[4096]{0:T(1024)S(1)}, f32[4096]{0:T(1024)}, u32[]{:S(2)}) copy-start(f32[4096]{0:T(1024)} %param.7) | copy-start | bytes 49156
  58.9 169.0 %all-reduce.11.cloned.1.call-start = ((), (), s32[]{:S(2)}) async-start(), calls=%async_computation.1 | async-start | bytes 2097152 | tf_op jit(solution)/shard_map/psum | solution.py:58
  166.4 61.6 %copy-start = (f32[2048,128]{1,0:T(8,128)S(1)}, f32[2048,128]{1,0:T(8,128)}, u32[]{:S(2)}) copy-start(f32[2048,128]{1,0:T(8,128)} %param.9) | copy-start | bytes 3145732
  176.8 206.4 %all-reduce.13.cloned.1.call-start = ((), (), s32[]{:S(2)}) async-start(), calls=%async_computation.2 | async-start | bytes 4194304 | tf_op jit(solution)/shard_map/psum | solution.py:50
  321.9 165.6 %all-reduce.15.cloned.1.call-start = ((), (), s32[]{:S(2)}) async-start(), calls=%async_computation.3 | async-start | bytes 2097152 | tf_op jit(solution)/shard_map/psum | solution.py:58
  436.4 207.4 %all-reduce.17.cloned.1.call-start = ((), (), s32[]{:S(2)}) async-start(), calls=%async_computation.4 | async-start | bytes 4194304 | tf_op jit(solution)/shard_map/psum | solution.py:50
  582.6 165.7 %all-reduce.19.cloned.1.call-start = ((), (), s32[]{:S(2)}) async-start(), calls=%async_computation.5 | async-start | bytes 2097152 | tf_op jit(solution)/shard_map/psum | solution.py:58
  686.6 104.3 %copy-start.1 = (f32[2048,128]{1,0:T(8,128)S(1)}, f32[2048,128]{1,0:T(8,128)}, u32[]{:S(2)}) copy-start(f32[2048,128]{1,0:T(8,128)} %get-tuple-element.21) | copy-start | bytes 3145732
Sparse Core Ops, SparseCore 0:
  59.0 64.4 all-reduce.8
  177.0 50.9 all-reduce.10
  322.0 61.1 all-reduce.12
  436.5 50.9 all-reduce.14
  582.7 61.0 all-reduce.16
  697.3 50.9 all-reduce.18
where the time goes:
time: 810 us; the launch traced here: 802 us
  waiting for transfers between devices  338 us (42%)
  local copies, waits for them, and re-layouts  162 us (20%)
  matrix products  141 us (17%)
  blocking collectives  121 us (15%)
  other arithmetic  24.7 us (3%)
  between operations  14.7 us (2%)
    psum x3, waiting for transfers between devices, on_device(): projected = lax.psum(partial_rows, 'col')  185 us
    psum x3, waiting for transfers between devices, on_device(): lax.psum(summed.reshape(feature_rows, directions), 'row')  153 us
    psum x2, blocking collectives, on_device(): lax.psum((jnp.sum(own_rows(direction) * own_image, axis=0), jnp.sum(own_r...  80.2 us
    dot_general x3, local copies, waits for them, and re-layouts, on_device(): jnp.einsum('bij,bjk->bik', x_blocks, picked_tiles, preferred_element_type...  52.4 us
    dot_general x3, local copies, waits for them, and re-layouts, on_device(): jnp.einsum('bji,bjk->bik', x_blocks, picked_rows, preferred_element_type=...  52.4 us
    dot_general x3, matrix products, on_device(): jnp.einsum('bji,bjk->bik', x_blocks, picked_rows, preferred_element_type=...  43.1 us
    psum x1, blocking collectives, on_device(): norm_now = lax.psum(jnp.sum(mine * mine, axis=0), ('row', 'col'))  40.4 us
    dot_general x3, matrix products, on_device(): jnp.einsum('bij,bjk->bik', x_blocks, picked_tiles, preferred_element_type...  38.5 us
  transfers between devices with their start and end apart: 6, of which 6 were waited for; matrix products, arithmetic and copies ran while one was open for 0% of the time, Pallas kernels for 0%

commit v1 on v0

--- a/solution.py
+++ b/solution.py
@@ -47,7 +47,11 @@
             "bij,bjk->bik", x_blocks, picked_tiles, preferred_element_type=jnp.float32
         )
         partial_rows = jnp.einsum("br,bik->rik", row_select, forward, precision=highest)
-        projected = lax.psum(partial_rows, "col")
+        projected = partial_rows
+        for hop in (1, 2, 4):
+            projected = projected + lax.ppermute(
+                projected, "col", [(dev, dev ^ hop) for dev in range(8)]
+            )
         scaled = (weights * projected).astype(jnp.bfloat16)
         picked_rows = scaled[block_row]
         backward = jnp.einsum(

time: 810 us -> 923 us (1.14)
  waiting for transfers between devices: 338 us -> 439 us
  starting transfers between devices: 0.88 us -> 13.9 us
    ppermute x0 -> x9, waiting for transfers between devices: none -> 284 us  [on_device(): lax.ppermute(projected, 'col', [(dev, dev ^ hop) for dev in range(8)])]
    psum x3 -> x0, waiting for transfers between devices: 185 us -> none  [on_device(): projected = lax.psum(partial_rows, 'col')]
    ppermute x0 -> x9, starting transfers between devices: none -> 13.7 us  [on_device(): lax.ppermute(projected, 'col', [(dev, dev ^ hop) for dev in range(8)])]
  transfers between devices with their start and end apart: 6 -> 12, of which waited for: 6 -> 12; matrix products, arithmetic and copies ran while one was open for 0% -> 0% of each run, Pallas kernels for 0% -> 0%
where the time goes in v1:
time: 923 us; the launch traced here: 913 us
  waiting for transfers between devices  439 us (48%)
  local copies, waits for them, and re-layouts  162 us (18%)
  matrix products  138 us (15%)
  blocking collectives  121 us (13%)
  other arithmetic  25.2 us (3%)
  between operations  14.4 us (2%)
  starting transfers between devices  13.9 us (2%)
    ppermute x9, waiting for transfers between devices, on_device(): lax.ppermute(projected, 'col', [(dev, dev ^ hop) for dev in range(8)])  284 us
    psum x3, waiting for transfers between devices, on_device(): lax.psum(summed.reshape(feature_rows, directions), 'row')  154 us
    psum x2, blocking collectives, on_device(): lax.psum((jnp.sum(own_rows(direction) * own_image, axis=0), jnp.sum(own_r...  80.2 us
    dot_general x3, local copies, waits for them, and re-layouts, on_device(): jnp.einsum('bij,bjk->bik', x_blocks, picked_tiles, preferred_element_type...  52.4 us
    dot_general x3, local copies, waits for them, and re-layouts, on_device(): jnp.einsum('bji,bjk->bik', x_blocks, picked_rows, preferred_element_type=...  52.4 us
    dot_general x3, matrix products, on_device(): jnp.einsum('bji,bjk->bik', x_blocks, picked_rows, preferred_element_type=...  43.1 us
    psum x1, blocking collectives, on_device(): norm_now = lax.psum(jnp.sum(mine * mine, axis=0), ('row', 'col'))  40.4 us
    dot_general x3, matrix products, on_device(): jnp.einsum('bij,bjk->bik', x_blocks, picked_tiles, preferred_element_type...  38.5 us
  transfers between devices with their start and end apart: 12, of which 12 were waited for; matrix products, arithmetic and copies ran while one was open for 0% of the time, Pallas kernels for 0%

profile of v1, /device:TPU:0, one launch (start us, length us, event | category | flops | bytes accessed | tf_op | source)
XLA Modules:
  0.0 913.3 jit_solution(5008541524430395979)
XLA Ops:
  17.8 12.8 %convolution_bitcast_fusion.5 = f32[256,128,128]{1,2,0:T(8,128)} fusion(bf16[256,128,128]{2,1,0:T(8,128)(2,1)} %gather_fusion, bf16[256,128,128]{2,1,0:T(8,128)(2,1)} %param.5), kind=kOutput, calls=%fused_computation.11 | convolution fusion | flops 1073741824 | bytes 33554432 | tf_op jit(solution)/shard_map/bij,bjk->bik/dot_general | solution.py:46
  30.6 17.5 %copy.32 = f32[256,128,128]{2,0,1:T(8,128)} copy(f32[256,128,128]{1,2,0:T(8,128)} %convolution_bitcast_fusion.5) | data formatting | bytes 33554432 | tf_op jit(solution)/shard_map/bij,bjk->bik/dot_general | solution.py:46
  65.6 45.9 %collective-permute-done.1 = f32[32,128,128]{2,0,1:T(8,128)S(1)} collective-permute-done((f32[32,128,128]{2,0,1:T(8,128)S(1)}, f32[32,128,128]{2,0,1:T(8,128)S(1)}, u32[]{:S(2)}, u32[]{:S(2)}) %collective-permute-start.1) | collective-permute-done | bytes 2097184 | tf_op jit(solution)/shard_map/ppermute | solution.py:52
  115.6 43.7 %collective-permute-done.2 = f32[32,128,128]{2,0,1:T(8,128)} collective-permute-done((f32[32,128,128]{2,0,1:T(8,128)S(1)}, f32[32,128,128]{2,0,1:T(8,128)}, u32[]{:S(2)}, u32[]{:S(2)}) %collective-permute-start.2) | collective-permute-done | bytes 2097184 | tf_op jit(solution)/shard_map/ppermute | solution.py:52
  170.5 14.4 %convolution_bitcast_fusion.4 = f32[256,128,128]{1,2,0:T(8,128)} fusion(bf16[256,128,128]{2,1,0:T(8,128)(2,1)} %gather_fusion.1, bf16[256,128,128]{2,1,0:T(8,128)(2,1)} %param.5), kind=kOutput, calls=%fused_computation.10 | convolution fusion | flops 1073741824 | bytes 33554432 | tf_op jit(solution)/shard_map/bji,bjk->bik/dot_general | solution.py:57
  184.9 17.5 %copy.35 = f32[256,128,128]{2,0,1:T(8,128)} copy(f32[256,128,128]{1,2,0:T(8,128)} %convolution_bitcast_fusion.4) | data formatting | bytes 33554432 | tf_op jit(solution)/shard_map/bji,bjk->bik/dot_general | solution.py:57
  212.9 53.2 %all-reduce.6.cloned.1.call-done = f32[2048,128]{1,0:T(8,128)} async-done(((f32[2048,128]{1,0:T(8,128)}), f32[2048,128]{1,0:T(8,128)}) %all-reduce.6.cloned.1.call-update) | async-done | bytes 1048592 | tf_op jit(solution)/shard_map/psum | solution.py:62
  267.5 40.4 %all-reduce.1 = (f32[128]{0:T(128)S(1)}, f32[128]{0:T(128)S(1)}, f32[128]{0:T(128)S(1)}) all-reduce(f32[128]{0:T(128)S(1)} %get-tuple-element.7, f32[128]{0:T(128)S(1)} %get-tuple-element.6, f32[128]{0:T(128)S(1)} %get-tuple-element.5), channel_id=1, replica_groups=mesh['row'=4,'col'=8] {'row','col'}, use_global_device_ids=true, to_apply=%region_1.2 | all-reduce | flops 384 | bytes 3072 | tf_op jit(solution)/shard_map/psum | solution.py:42
  319.0 12.8 %convolution_bitcast_fusion.3 = f32[256,128,128]{1,2,0:T(8,128)} fusion(bf16[256,128,128]{2,1,0:T(8,128)(2,1)} %gather_fusion.2, bf16[256,128,128]{2,1,0:T(8,128)(2,1)} %param.5), kind=kOutput, calls=%fused_computation.9 | convolution fusion | flops 1073741824 | bytes 33554432 | tf_op jit(solution)/shard_map/bij,bjk->bik/dot_general | solution.py:46
  331.8 17.5 %copy.38 = f32[256,128,128]{2,0,1:T(8,128)} copy(f32[256,128,128]{1,2,0:T(8,128)} %convolution_bitcast_fusion.3) | data formatting | bytes 33554432 | tf_op jit(solution)/shard_map/bij,bjk->bik/dot_general | solution.py:46
  366.1 45.9 %collective-permute-done.4 = f32[32,128,128]{2,0,1:T(8,128)S(1)} collective-permute-done((f32[32,128,128]{2,0,1:T(8,128)S(1)}, f32[32,128,128]{2,0,1:T(8,128)S(1)}, u32[]{:S(2)}, u32[]{:S(2)}) %collective-permute-start.4) | collective-permute-done | bytes 2097184 | tf_op jit(solution)/shard_map/ppermute | solution.py:52
  414.3 45.4 %collective-permute-done.5 = f32[32,128,128]{2,0,1:T(8,128)S(1)} collective-permute-done((f32[32,128,128]{2,0,1:T(8,128)S(1)}, f32[32,128,128]{2,0,1:T(8,128)S(1)}, u32[]{:S(2)}, u32[]{:S(2)}) %collective-permute-start.5) | collective-permute-done | bytes 2097184 | tf_op jit(solution)/shard_map/ppermute | solution.py:52
  469.6 14.4 %convolution_bitcast_fusion.2 = f32[256,128,128]{1,2,0:T(8,128)} fusion(bf16[256,128,128]{2,1,0:T(8,128)(2,1)} %gather_fusion.3, bf16[256,128,128]{2,1,0:T(8,128)(2,1)} %param.5), kind=kOutput, calls=%fused_computation.8 | convolution fusion | flops 1073741824 | bytes 33554432 | tf_op jit(solution)/shard_map/bji,bjk->bik/dot_general | solution.py:57
  484.0 17.5 %copy.41 = f32[256,128,128]{2,0,1:T(8,128)} copy(f32[256,128,128]{1,2,0:T(8,128)} %convolution_bitcast_fusion.2) | data formatting | bytes 33554432 | tf_op jit(solution)/shard_map/bji,bjk->bik/dot_general | solution.py:57
  511.9 50.5 %all-reduce.8.cloned.1.call-done = f32[2048,128]{1,0:T(8,128)} async-done(((f32[2048,128]{1,0:T(8,128)}), f32[2048,128]{1,0:T(8,128)}) %all-reduce.8.cloned.1.call-update) | async-done | bytes 1048592 | tf_op jit(solution)/shard_map/psum | solution.py:62
  564.8 40.2 %all-reduce = (f32[128]{0:T(128)S(1)}, f32[128]{0:T(128)S(1)}, f32[128]{0:T(128)S(1)}) all-reduce(f32[128]{0:T(128)S(1)} %get-tuple-element.3, f32[128]{0:T(128)S(1)} %get-tuple-element.4, f32[128]{0:T(128)S(1)} %get-tuple-element.2), channel_id=1, replica_groups=mesh['row'=4,'col'=8] {'row','col'}, use_global_device_ids=true, to_apply=%region_14.15 | all-reduce | flops 384 | bytes 3072 | tf_op jit(solution)/shard_map/psum | solution.py:66
  616.4 12.8 %convolution_bitcast_fusion.1 = f32[256,128,128]{1,2,0:T(8,128)} fusion(bf16[256,128,128]{2,1,0:T(8,128)(2,1)} %gather_fusion.4, bf16[256,128,128]{2,1,0:T(8,128)(2,1)} %param.5), kind=kOutput, calls=%fused_computation.7 | convolution fusion | flops 1073741824 | bytes 33554432 | tf_op jit(solution)/shard_map/bij,bjk->bik/dot_general | solution.py:46
  629.2 17.5 %copy.44 = f32[256,128,128]{2,0,1:T(8,128)} copy(f32[256,128,128]{1,2,0:T(8,128)} %convolution_bitcast_fusion.1) | data formatting | bytes 33554432 | tf_op jit(solution)/shard_map/bij,bjk->bik/dot_general | solution.py:46
  663.5 45.9 %collective-permute-done.7 = f32[32,128,128]{2,0,1:T(8,128)S(1)} collective-permute-done((f32[32,128,128]{2,0,1:T(8,128)S(1)}, f32[32,128,128]{2,0,1:T(8,128)S(1)}, u32[]{:S(2)}, u32[]{:S(2)}) %collective-permute-start.7) | collective-permute-done | bytes 2097184 | tf_op jit(solution)/shard_map/ppermute | solution.py:52
  711.7 45.4 %collective-permute-done.8 = f32[32,128,128]{2,0,1:T(8,128)S(1)} collective-permute-done((f32[32,128,128]{2,0,1:T(8,128)S(1)}, f32[32,128,128]{2,0,1:T(8,128)S(1)}, u32[]{:S(2)}, u32[]{:S(2)}) %collective-permute-start.8) | collective-permute-done | bytes 2097184 | tf_op jit(solution)/shard_map/ppermute | solution.py:52
  767.1 14.4 %convolution_bitcast_fusion = f32[256,128,128]{1,2,0:T(8,128)} fusion(bf16[256,128,128]{2,1,0:T(8,128)(2,1)} %gather_fusion.5, bf16[256,128,128]{2,1,0:T(8,128)(2,1)} %param.5), kind=kOutput, calls=%fused_computation.6 | convolution fusion | flops 1073741824 | bytes 33554432 | tf_op jit(solution)/shard_map/bji,bjk->bik/dot_general | solution.py:57
  781.5 17.5 %copy.47 = f32[256,128,128]{2,0,1:T(8,128)} copy(f32[256,128,128]{1,2,0:T(8,128)} %convolution_bitcast_fusion) | data formatting | bytes 33554432 | tf_op jit(solution)/shard_map/bji,bjk->bik/dot_general | solution.py:57
  809.4 50.6 %all-reduce.10.cloned.1.call-done = f32[2048,128]{1,0:T(8,128)} async-done(((f32[2048,128]{1,0:T(8,128)}), f32[2048,128]{1,0:T(8,128)}) %all-reduce.10.cloned.1.call-update) | async-done | bytes 1048592 | tf_op jit(solution)/shard_map/psum | solution.py:62
  862.7 40.0 %psum.82 = f32[128]{0:T(128)S(1)} all-reduce(f32[128]{0:T(128)S(1)} %multiply_reduce_fusion), channel_id=1, replica_groups=mesh['row'=4,'col'=8] {'row','col'}, use_global_device_ids=true, to_apply=%region_17.18 | all-reduce | flops 128 | bytes 1024 | tf_op jit(solution)/shard_map/psum | solution.py:66
  (74 shorter events, 165.3 us)
Async XLA Ops:
  7.2 258.9 %all-reduce.6.cloned.1.call-start = ((), (), s32[]{:S(2)}) async-start(), calls=%async_computation | async-start | bytes 2097152 | tf_op jit(solution)/shard_map/psum | solution.py:62
  57.9 56.0 %copy-start.3 = (s32[512]{0:T(512)S(1)}, s32[512]{0:T(512)}, u32[]{:S(2)}) copy-start(s32[512]{0:T(512)} %param.8) | copy-start | bytes 6148
  57.9 57.5 %copy-start.2 = (f32[4096]{0:T(1024)S(1)}, f32[4096]{0:T(1024)}, u32[]{:S(2)}) copy-start(f32[4096]{0:T(1024)} %param.7) | copy-start | bytes 49156
  57.9 4.4 collective-permute-start
  62.7 48.8 %collective-permute-start.1 = (f32[32,128,128]{2,0,1:T(8,128)S(1)}, f32[32,128,128]{2,0,1:T(8,128)S(1)}, u32[]{:S(2)}, u32[]{:S(2)}) collective-permute-start(f32[32,128,128]{2,0,1:T(8,128)S(1)} %add.128), channel_id=1, source_target_pairs={{0,2},{1,3},{2,0},{3,1},{4,6},{5,7},{6,4},{7,5},{8,10},{9,11},{10,... | collective-permute-start | bytes 6291464 | tf_op jit(solution)/shard_map/ppermute | solution.py:52
  112.1 47.3 %collective-permute-start.2 = (f32[32,128,128]{2,0,1:T(8,128)S(1)}, f32[32,128,128]{2,0,1:T(8,128)}, u32[]{:S(2)}, u32[]{:S(2)}) collective-permute-start(f32[32,128,128]{2,0,1:T(8,128)S(1)} %add.129), channel_id=1, source_target_pairs={{0,4},{1,5},{2,6},{3,7},{4,0},{5,1},{6,2},{7,3},{8,12},{9,13},{10,... | collective-permute-start | bytes 6291464 | tf_op jit(solution)/shard_map/ppermute | solution.py:52
  202.4 63.7 %copy-start = (f32[2048,128]{1,0:T(8,128)S(1)}, f32[2048,128]{1,0:T(8,128)}, u32[]{:S(2)}) copy-start(f32[2048,128]{1,0:T(8,128)} %param.9) | copy-start | bytes 3145732
  212.8 349.6 %all-reduce.8.cloned.1.call-start = ((), (), s32[]{:S(2)}) async-start(), calls=%async_computation.1 | async-start | bytes 2097152 | tf_op jit(solution)/shard_map/psum | solution.py:62
  359.0 4.2 collective-permute-start.3
  363.8 48.3 %collective-permute-start.4 = (f32[32,128,128]{2,0,1:T(8,128)S(1)}, f32[32,128,128]{2,0,1:T(8,128)S(1)}, u32[]{:S(2)}, u32[]{:S(2)}) collective-permute-start(f32[32,128,128]{2,0,1:T(8,128)S(1)} %add.135), channel_id=1, source_target_pairs={{0,2},{1,3},{2,0},{3,1},{4,6},{5,7},{6,4},{7,5},{8,10},{9,11},{10,... | collective-permute-start | bytes 6291464 | tf_op jit(solution)/shard_map/ppermute | solution.py:52
  412.5 47.2 %collective-permute-start.5 = (f32[32,128,128]{2,0,1:T(8,128)S(1)}, f32[32,128,128]{2,0,1:T(8,128)S(1)}, u32[]{:S(2)}, u32[]{:S(2)}) collective-permute-start(f32[32,128,128]{2,0,1:T(8,128)S(1)} %add.136), channel_id=1, source_target_pairs={{0,4},{1,5},{2,6},{3,7},{4,0},{5,1},{6,2},{7,3},{8,12},{9,13},{10,... | collective-permute-start | bytes 6291464 | tf_op jit(solution)/shard_map/ppermute | solution.py:52
  511.8 348.2 %all-reduce.10.cloned.1.call-start = ((), (), s32[]{:S(2)}) async-start(), calls=%async_computation.2 | async-start | bytes 2097152 | tf_op jit(solution)/shard_map/psum | solution.py:62
  656.4 4.2 collective-permute-start.6
  661.1 48.3 %collective-permute-start.7 = (f32[32,128,128]{2,0,1:T(8,128)S(1)}, f32[32,128,128]{2,0,1:T(8,128)S(1)}, u32[]{:S(2)}, u32[]{:S(2)}) collective-permute-start(f32[32,128,128]{2,0,1:T(8,128)S(1)} %add.142), channel_id=1, source_target_pairs={{0,2},{1,3},{2,0},{3,1},{4,6},{5,7},{6,4},{7,5},{8,10},{9,11},{10,... | collective-permute-start | bytes 6291464 | tf_op jit(solution)/shard_map/ppermute | solution.py:52
  709.9 47.2 %collective-permute-start.8 = (f32[32,128,128]{2,0,1:T(8,128)S(1)}, f32[32,128,128]{2,0,1:T(8,128)S(1)}, u32[]{:S(2)}, u32[]{:S(2)}) collective-permute-start(f32[32,128,128]{2,0,1:T(8,128)S(1)} %add.143), channel_id=1, source_target_pairs={{0,4},{1,5},{2,6},{3,7},{4,0},{5,1},{6,2},{7,3},{8,12},{9,13},{10,... | collective-permute-start | bytes 6291464 | tf_op jit(solution)/shard_map/ppermute | solution.py:52
  798.9 103.7 %copy-start.1 = (f32[2048,128]{1,0:T(8,128)S(1)}, f32[2048,128]{1,0:T(8,128)}, u32[]{:S(2)}) copy-start(f32[2048,128]{1,0:T(8,128)} %get-tuple-element.21) | copy-start | bytes 3145732
Sparse Core Ops, SparseCore 0:
  212.9 53.1 all-reduce.5
  512.0 50.3 all-reduce.7
  809.6 50.3 all-reduce.9
